TPU v7x, 32 devices: a whole 2x2x4 slice. The times are simulated.
32 devices in a mesh: seq: 4 (over z), tp: 8 (over y, x, core).
Axes of the slice: x: 2, y: 2, z: 4, core: 2. Of those that a mesh axis runs over, the one named last changes fastest.
Arguments:
- tokens: bfloat16 [1024, 8192], P('tp', 'seq'), may hold values from -6 to 6
- gate_weight: bfloat16 [8192, 14336], P('seq', 'tp'), may hold values from -0.0625 to 0.0625
- up_weight: bfloat16 [8192, 14336], P('seq', 'tp'), may hold values from -0.0625 to 0.0625
- down_pool: bfloat16 [64, 64, 8192], P('tp', None, 'seq'), may hold values from -0.0625 to 0.0625
- up_pool: bfloat16 [64, 2, 64, 14336], P('seq', None, None, 'tp'), may hold values from -0.75 to 0.75
- req_len: int32 [4], replicated, may hold values from 1 to 4, 8 in all
- req_adapter: int32 [4], replicated, may hold values from 0 to 63
- owner_slot: int32 [64], replicated, may hold values from 0 to 63, each once
Outputs:
- hidden: bfloat16 [1024, 14336], P('seq', 'tp')
Inputs may be any that keep to these rules, and one draw needn't show every extreme that they name: `req_len`: lengths of the requests in segments, summing to 8; the longest is exactly 4. `req_adapter`: adapter ids; an adapter may serve several requests. `owner_slot`: each pool slot once.
All inputs are finite; a program needn't handle non-finite values.
Results may differ from a plain program's by a relative error of at most 0.015.
Values may be sent and summed in bfloat16 or wider, within the bound.
No kernel may reach another device: no remote copies, remote signals or barrier semaphores. Data moves between devices by JAX's collectives and lax.ppermute only.
A program may use at most 128 MiB of HBM per device.

v0:
```python
import jax
import jax.numpy as jnp
from jax import lax
from jax.sharding import PartitionSpec as P

SEG_ROWS = 128
low_rank_scale = 0.5


def segment_slots(req_len, req_adapter, owner_slot, segs):
    ends = jnp.cumsum(req_len)
    segment = jnp.arange(segs, dtype=jnp.int32)
    seg_request = jnp.sum((ends[None, :] <= segment[:, None]).astype(jnp.int32), axis=1)
    return jnp.take(owner_slot, jnp.take(req_adapter, seg_request))


def shards(tokens, gate_weight, up_weight, down_pool, up_pool, req_len, req_adapter, owner_slot):
    nseq = lax.axis_size("seq")
    ntp = lax.axis_size("tp")
    segs = tokens.shape[0] // SEG_ROWS * ntp
    seg_slot = segment_slots(req_len, req_adapter, owner_slot, segs)
    per_tp = down_pool.shape[0]
    per_seq = up_pool.shape[0]
    width = tokens.shape[1]
    half_width = gate_weight.shape[1]
    rank_size = down_pool.shape[1]
    own_segs = segs // nseq
    own_rows = own_segs * SEG_ROWS
    held_down = seg_slot // per_tp == lax.axis_index("tp")
    picked_down = jnp.take(down_pool, seg_slot % per_tp, axis=0).astype(jnp.float32)
    table_down = jnp.where(held_down[:, None, None], picked_down, 0.0)
    downs = lax.psum(table_down.astype(jnp.bfloat16), "tp")
    held_up = seg_slot // per_seq == lax.axis_index("seq")
    picked_up = jnp.take(up_pool, seg_slot % per_seq, axis=0).astype(jnp.float32)
    table_up = jnp.where(held_up[:, None, None, None], picked_up, 0.0)
    ups_own = lax.psum_scatter(
        table_up.astype(jnp.bfloat16), "seq", scatter_dimension=0, tiled=True
    )
    gathered = lax.all_gather(tokens, "tp", axis=0, tiled=True)
    inner_part = jnp.einsum(
        "kqd,krd->kqr",
        gathered.reshape(segs, SEG_ROWS, width),
        downs,
        preferred_element_type=jnp.float32,
    )
    inner_part = lax.optimization_barrier(inner_part.astype(jnp.bfloat16)).astype(jnp.float32)
    flat = inner_part.reshape(-1, 128)
    flat_own = own_rows * rank_size // 128
    inner_total = lax.psum(flat.astype(jnp.bfloat16), "seq").astype(jnp.float32)
    inner_own = lax.dynamic_slice_in_dim(inner_total, lax.axis_index("seq") * flat_own, flat_own, 0)
    inner_iteration = inner_own.astype(jnp.bfloat16).reshape(own_segs, SEG_ROWS, rank_size)
    low_rank_delta = jnp.einsum(
        "vcz,vwzd->vcwd", inner_iteration, ups_own, preferred_element_type=jnp.float32
    ).reshape(own_rows, 2, half_width)
    reduced_total = lax.psum_scatter(
        jnp.concatenate(
            [
                jnp.dot(gathered, gate_weight, preferred_element_type=jnp.float32),
                jnp.dot(gathered, up_weight, preferred_element_type=jnp.float32),
            ],
            axis=1,
        ).astype(jnp.bfloat16),
        "seq",
        scatter_dimension=0,
        tiled=True,
    ).astype(jnp.float32)
    gate_preactivation = reduced_total[:, :half_width] + low_rank_scale * low_rank_delta[:, 0]
    up_preactivation = reduced_total[:, half_width:] + low_rank_scale * low_rank_delta[:, 1]
    return (jax.nn.silu(gate_preactivation) * up_preactivation).astype(jnp.bfloat16)


def solution(mesh):
    placed = (
        P("tp", "seq"),
        P("seq", "tp"),
        P("seq", "tp"),
        P("tp", None, "seq"),
        P("seq", None, None, "tp"),
        P(),
        P(),
        P(),
    )
    return jax.shard_map(
        shards, mesh=mesh, in_specs=placed, out_specs=P("seq", "tp"), check_vma=False
    )
```

profile of v0, /device:TPU:0, one launch (start us, length us, event | category | flops | bytes accessed | tf_op | source)
XLA Modules:
  0.0 369.6 jit_solution(8576012177038805279)
XLA Ops:
  6.5 0.0 copy-start
  6.5 0.0 all-reduce.3.cloned.1.call-start
  6.5 1.0 reduce-window.8
  7.5 0.1 convert_reduce_fusion
  7.6 1.3 gather_fusion
  8.9 1.3 gather_fusion.1
  10.3 0.0 copy-done
  10.3 2.0 gather_fusion.2
  12.4 3.6 select_convert_fusion.1
  16.0 0.0 all-reduce.3.cloned.1.call-update
  16.0 0.0 all-gather.2.cloned.1.call-start
  16.1 0.7 all-gather.2.cloned.1.call-update
  16.8 0.0 all-reduce.5.cloned.1.call-start
  16.9 5.8 %gather_fusion.3 = bf16[8,2,64,1792]{3,2,1,0:T(8,128)(2,1)} fusion(bf16[16,2,64,1792]{3,2,1,0:T(8,128)(2,1)} %param.12, s32[1024]{0:T(1024)S(1)} %pad_clamp_fusion), kind=kCustom, calls=%fused_computation.3 | custom fusion | bytes 7340064 | tf_op jit(solution)/shard_map/jit(_take)/gather | solution.py:34
  22.6 57.7 %all-reduce.3.cloned.1.call-done = bf16[8,64,2048]{2,1,0:T(8,128)(2,1)} async-done(((bf16[8,64,2048]{2,1,0:T(8,128)(2,1)}), bf16[8,64,2048]{2,1,0:T(8,128)(2,1)}) %all-reduce.3.cloned.1.call-update) | async-done | bytes 2097168 | tf_op jit(solution)/shard_map/psum | solution.py:32
  80.3 37.8 %all-gather.2.cloned.1.call-done = bf16[1024,2048]{1,0:T(8,128)(2,1)} async-done(((bf16[128,2048]{1,0:T(8,128)(2,1)}), bf16[1024,2048]{1,0:T(8,128)(2,1)}) %all-gather.2.cloned.1.call-update) | async-done | bytes 4194320 | tf_op jit(solution)/shard_map/all_gather | solution.py:39
  118.2 4.4 %fusion.6 = bf16[8,128,64]{1,2,0:T(8,128)(2,1)S(1)} fusion(bf16[8,64,2048]{2,1,0:T(8,128)(2,1)} %all-reduce.3.cloned.1.call-done, bf16[8,128,2048]{2,1,0:T(8,128)(2,1)} %bitcast.61), kind=kOutput, calls=%fused_computation.18 | convolution fusion | flops 268500992 | bytes 6422528 | tf_op jit(solution)/shard_map/kqd,krd->kqr/dot_general | solution.py:40
  122.5 0.2 copy.13
  122.7 0.8 convert_element_type.45
  123.5 0.0 all-reduce.5.cloned.1.call-update
  123.6 0.0 reduce-scatter.5.cloned.1.call-start
  123.6 4.9 %select_convert_fusion = bf16[8,2,64,1792]{3,2,1,0:T(8,128)(2,1)} fusion(bf16[8,2,64,1792]{3,2,1,0:T(8,128)(2,1)} %gather_fusion.3, pred[8]{0:T(512)(128)(4,1)S(1)} %get-tuple-element.10, pred[8]{0:T(512)(128)(4,1)S(1)} %get-tuple-element.11), kind=kLoop, calls=%fused_computation.5 | loop fusion | flops 7340032 | bytes 7340048 | tf_op jit(solution)/shard_map/convert_element_type | solution.py:37
  128.6 0.0 reduce-scatter.5.cloned.1.call-update
  128.6 0.0 reduce-scatter.3.cloned.1.call-start
  128.6 0.0 copy-start.3
  128.6 13.1 %convolution_convert_fusion = bf16[1024,1792]{1,0:T(8,128)(2,1)} fusion(bf16[1024,2048]{1,0:T(8,128)(2,1)} %all-gather.2.cloned.1.call-done, bf16[2048,1792]{1,0:T(8,128)(2,1)} %param.10), kind=kOutput, calls=%fused_computation.7 | convolution fusion | flops 7518027776 | bytes 15204352 | tf_op jit(solution)/shard_map/dot_general | solution.py:59
  141.7 0.0 copy-done.3
  141.7 12.3 %convolution_convert_fusion.1 = bf16[1024,1792]{1,0:T(8,128)(2,1)} fusion(bf16[1024,2048]{1,0:T(8,128)(2,1)S(1)} %copy-done.3, bf16[2048,1792]{1,0:T(8,128)(2,1)} %param.9), kind=kOutput, calls=%fused_computation.8 | convolution fusion | flops 7518027776 | bytes 15204352 | tf_op jit(solution)/shard_map/dot_general | solution.py:58
  154.0 6.6 %pad_maximum_fusion = bf16[1024,3584]{1,0:T(8,128)(2,1)} fusion(bf16[1024,1792]{1,0:T(8,128)(2,1)} %convolution_convert_fusion, bf16[1024,1792]{1,0:T(8,128)(2,1)} %convolution_convert_fusion.1), kind=kLoop, calls=%fused_computation.4 | loop fusion | flops 14680064 | bytes 14680064 | tf_op jit(solution)/shard_map/concatenate | solution.py:56
  160.6 0.0 reduce-scatter.3.cloned.1.call-update
  160.6 0.0 all-reduce.5.cloned.1.call-done
  160.6 0.8 convert_convert_fusion
  161.4 0.1 reshape.295
  161.5 67.0 %reduce-scatter.5.cloned.1.call-done = bf16[2,2,64,1792]{3,2,1,0:T(8,128)(2,1)} async-done(((bf16[8,2,64,1792]{3,2,1,0:T(8,128)(2,1)}), bf16[2,2,64,1792]{3,2,1,0:T(8,128)(2,1)}) %reduce-scatter.5.cloned.1.call-update) | async-done | bytes 917520 | tf_op jit(solution)/shard_map/reduce_scatter | solution.py:36
  228.5 3.7 %fusion.7 = f32[2,128,2,1792]{3,1,0,2:T(8,128)} fusion(bf16[2,2,64,1792]{3,2,1,0:T(8,128)(2,1)} %reduce-scatter.5.cloned.1.call-done, bf16[2,128,64]{2,1,0:T(8,128)(2,1)S(1)} %reshape.295), kind=kOutput, calls=%fused_computation.19 | convolution fusion | flops 117440512 | bytes 4620288 | tf_op jit(solution)/shard_map/vcz,vwzd->vcwd/dot_general | solution.py:52
  232.2 126.7 %reduce-scatter.3.cloned.1.call-done = bf16[256,3584]{1,0:T(8,128)(2,1)} async-done(((bf16[1024,3584]{1,0:T(8,128)(2,1)}), bf16[256,3584]{1,0:T(8,128)(2,1)}) %reduce-scatter.3.cloned.1.call-update) | async-done | bytes 1835024 | tf_op jit(solution)/shard_map/reduce_scatter | solution.py:55
  358.9 0.0 copy-start.2
  358.9 2.1 convert_element_type.39
  361.0 0.0 copy-start.1
  361.0 0.5 copy-done.2
  361.5 1.6 fusion.3
  363.0 0.0 copy-done.1
  (10 shorter events, 0.1 us)
Async XLA Ops:
  6.5 3.8 %copy-start = (bf16[8,64,2048]{2,1,0:T(8,128)(2,1)S(1)}, bf16[8,64,2048]{2,1,0:T(8,128)(2,1)}, u32[]{:S(2)}) copy-start(bf16[8,64,2048]{2,1,0:T(8,128)(2,1)} %param.11) | copy-start | bytes 6291460
  6.5 73.8 %all-reduce.3.cloned.1.call-start = ((), (), s32[]{:S(2)}) async-start(), calls=%async_computation.4 | async-start | bytes 4194304 | tf_op jit(solution)/shard_map/psum | solution.py:32
  16.0 102.1 %all-gather.2.cloned.1.call-start = ((), (), s32[]{:S(2)}) async-start(), calls=%async_computation.2 | async-start | bytes 4718592 | tf_op jit(solution)/shard_map/all_gather | solution.py:39
  16.8 143.9 %all-reduce.5.cloned.1.call-start = ((), (), s32[]{:S(2)}) async-start(), calls=%async_computation.5 | async-start | bytes 262144 | tf_op jit(solution)/shard_map/psum | solution.py:49
  123.6 104.9 %reduce-scatter.5.cloned.1.call-start = ((), (), s32[]{:S(2)}) async-start(), calls=%async_computation.6 | async-start | bytes 4587520 | tf_op jit(solution)/shard_map/reduce_scatter | solution.py:36
  128.6 230.3 %reduce-scatter.3.cloned.1.call-start = ((), (), s32[]{:S(2)}) async-start(), calls=%async_computation.3 | async-start | bytes 9175040 | tf_op jit(solution)/shard_map/reduce_scatter | solution.py:55
  128.6 13.1 %copy-start.3 = (bf16[1024,2048]{1,0:T(8,128)(2,1)S(1)}, bf16[1024,2048]{1,0:T(8,128)(2,1)}, u32[]{:S(2)}) copy-start(bf16[1024,2048]{1,0:T(8,128)(2,1)} %all-gather.2.cloned.1.call-done) | copy-start | bytes 12582916
  358.9 2.6 copy-start.2
  361.0 2.1 copy-start.1
Sparse Core Ops, SparseCore 0:
  16.2 64.1 all-reduce.2
  82.2 35.9 all-gather.1
  123.7 34.4 all-reduce.4
  160.4 68.0 reduce-scatter.4
  230.7 128.1 reduce-scatter.2
where the time goes:
time: 370 us
  waiting for transfers between devices  290 us (78%)
  matrix products  33.4 us (9%)
  other arithmetic  20.8 us (6%)
  between operations  13.3 us (4%)
  local copies, waits for them, and re-layouts  12 us (3%)
    reduce_scatter x1, waiting for transfers between devices, shards(): lax.psum_scatter(jnp.concatenate([jnp.dot(gathered, gate_weight, preferre...  127 us
    reduce_scatter x1, waiting for transfers between devices, shards(): lax.psum_scatter(table_up.astype(jnp.bfloat16), 'seq', scatter_dimension=...  67 us
    psum x1, waiting for transfers between devices, shards(): downs = lax.psum(table_down.astype(jnp.bfloat16), 'tp')  57.7 us
    all_gather x1, waiting for transfers between devices, shards(): gathered = lax.all_gather(tokens, 'tp', axis=0, tiled=True)  37.8 us
    dot_general x1, matrix products, shards(): jnp.dot(gathered, up_weight, preferred_element_type=jnp.float32)  13.1 us
    dot_general x1, matrix products, shards(): jnp.dot(gathered, gate_weight, preferred_element_type=jnp.float32)  12.3 us
  transfers between devices with their start and end apart: 5, of which 4 were waited for; matrix products, arithmetic and copies ran while one was open for 13% of the time, Pallas kernels for 0%

commit v1 on v0

--- a/solution.py
+++ b/solution.py
@@ -29,7 +29,7 @@
     held_down = seg_slot // per_tp == lax.axis_index("tp")
     picked_down = jnp.take(down_pool, seg_slot % per_tp, axis=0).astype(jnp.float32)
     table_down = jnp.where(held_down[:, None, None], picked_down, 0.0)
-    downs = lax.psum(table_down.astype(jnp.bfloat16), "tp")
+    downs = jnp.sum(lax.all_gather(table_down.astype(jnp.bfloat16), "tp"), axis=0)
     held_up = seg_slot // per_seq == lax.axis_index("seq")
     picked_up = jnp.take(up_pool, seg_slot % per_seq, axis=0).astype(jnp.float32)
     table_up = jnp.where(held_up[:, None, None, None], picked_up, 0.0)

time: 370 us -> 389 us (1.051)
  other arithmetic: 20.8 us -> 32.2 us
  waiting for transfers between devices: 290 us -> 300 us
    psum x1 -> x0, waiting for transfers between devices: 57.7 us -> none  [shards(): downs = lax.psum(table_down.astype(jnp.bfloat16), 'tp')]
    all_gather x0 -> x1, waiting for transfers between devices: none -> 53.9 us  [shards(): lax.all_gather(table_down.astype(jnp.bfloat16), 'tp')]
    psum x1, waiting for transfers between devices: 0.02 us -> 33.5 us  [shards(): inner_total = lax.psum(flat.astype(jnp.bfloat16), 'seq').astype(jnp.float32)]
    reduce_scatter x1, waiting for transfers between devices: 127 us -> 110 us  [shards(): lax.psum_scatter(jnp.concatenate([jnp.dot(gathered, gate_weight, preferre...]
    reduce_sum x0 -> x1, other arithmetic: none -> 9.96 us  [shards(): jnp.sum(lax.all_gather(table_down.astype(jnp.bfloat16), 'tp'), axis=0)]
    all_gather x1, waiting for transfers between devices: 37.8 us -> 32 us  [shards(): gathered = lax.all_gather(tokens, 'tp', axis=0, tiled=True)]
  transfers between devices with their start and end apart: 5 -> 5, of which waited for: 4 -> 5; matrix products, arithmetic and copies ran while one was open for 13% -> 18% of each run, Pallas kernels for 0% -> 0%
where the time goes in v1:
time: 389 us; the launch traced here: 388 us
  waiting for transfers between devices  300 us (77%)
  other arithmetic  32.2 us (8%)
  matrix products  31.2 us (8%)
  between operations  13.2 us (3%)
  local copies, waits for them, and re-layouts  11.8 us (3%)
    reduce_scatter x1, waiting for transfers between devices, shards(): lax.psum_scatter(jnp.concatenate([jnp.dot(gathered, gate_weight, preferre...  110 us
    reduce_scatter x1, waiting for transfers between devices, shards(): lax.psum_scatter(table_up.astype(jnp.bfloat16), 'seq', scatter_dimension=...  69.5 us
    all_gather x1, waiting for transfers between devices, shards(): lax.all_gather(table_down.astype(jnp.bfloat16), 'tp')  53.9 us
    psum x1, waiting for transfers between devices, shards(): inner_total = lax.psum(flat.astype(jnp.bfloat16), 'seq').astype(jnp.float32)  33.5 us
    all_gather x1, waiting for transfers between devices, shards(): gathered = lax.all_gather(tokens, 'tp', axis=0, tiled=True)  32 us
    dot_general x1, matrix products, shards(): jnp.dot(gathered, up_weight, preferred_element_type=jnp.float32)  13 us
    dot_general x1, matrix products, shards(): jnp.dot(gathered, gate_weight, preferred_element_type=jnp.float32)  12.4 us
    reduce_sum x1, other arithmetic, shards(): jnp.sum(lax.all_gather(table_down.astype(jnp.bfloat16), 'tp'), axis=0)  9.96 us
  transfers between devices with their start and end apart: 5, of which 5 were waited for; matrix products, arithmetic and copies ran while one was open for 18% of the time, Pallas kernels for 0%

profile of v1, /device:TPU:0, one launch (start us, length us, event | category | flops | bytes accessed | tf_op | source)
XLA Modules:
  0.0 388.5 jit_solution(17335427273976487903)
XLA Ops:
  6.5 0.0 copy-start
  6.5 0.0 all-gather.3.cloned.1.call-start
  6.5 0.7 all-gather.3.cloned.1.call-update
  7.3 0.0 all-gather.5.cloned.1.call-start
  7.3 0.8 reduce-window.8
  8.1 0.1 convert_reduce_fusion
  8.2 1.3 gather_fusion
  9.6 1.3 gather_fusion.1
  10.9 0.0 copy-done
  10.9 2.1 gather_fusion.2
  13.0 3.6 select_convert_fusion.1
  16.7 0.0 all-gather.5.cloned.1.call-update
  16.7 0.0 reduce-scatter.3.cloned.1.call-start
  16.7 32.0 %all-gather.3.cloned.1.call-done = bf16[1024,2048]{1,0:T(8,128)(2,1)} async-done(((bf16[128,2048]{1,0:T(8,128)(2,1)}), bf16[1024,2048]{1,0:T(8,128)(2,1)}) %all-gather.3.cloned.1.call-update) | async-done | bytes 4194320 | tf_op jit(solution)/shard_map/all_gather | solution.py:39
  48.7 0.0 copy-start.3
  48.7 13.0 %convolution_convert_fusion = bf16[1024,1792]{1,0:T(8,128)(2,1)} fusion(bf16[1024,2048]{1,0:T(8,128)(2,1)} %all-gather.3.cloned.1.call-done, bf16[2048,1792]{1,0:T(8,128)(2,1)} %param.10), kind=kOutput, calls=%fused_computation.7 | convolution fusion | flops 7518027776 | bytes 15204352 | tf_op jit(solution)/shard_map/dot_general | solution.py:59
  61.7 0.0 copy-done.3
  61.7 12.4 %convolution_convert_fusion.1 = bf16[1024,1792]{1,0:T(8,128)(2,1)} fusion(bf16[1024,2048]{1,0:T(8,128)(2,1)S(1)} %copy-done.3, bf16[2048,1792]{1,0:T(8,128)(2,1)} %param.9), kind=kOutput, calls=%fused_computation.8 | convolution fusion | flops 7518027776 | bytes 15204352 | tf_op jit(solution)/shard_map/dot_general | solution.py:58
  74.1 6.6 %pad_maximum_fusion = bf16[1024,3584]{1,0:T(8,128)(2,1)} fusion(bf16[1024,1792]{1,0:T(8,128)(2,1)} %convolution_convert_fusion, bf16[1024,1792]{1,0:T(8,128)(2,1)} %convolution_convert_fusion.1), kind=kLoop, calls=%fused_computation.4 | loop fusion | flops 14680064 | bytes 14680064 | tf_op jit(solution)/shard_map/concatenate | solution.py:56
  80.8 0.0 reduce-scatter.3.cloned.1.call-update
  80.8 0.0 all-reduce.2.cloned.1.call-start
  80.9 5.7 %gather_fusion.3 = bf16[8,2,64,1792]{3,2,1,0:T(8,128)(2,1)} fusion(bf16[16,2,64,1792]{3,2,1,0:T(8,128)(2,1)} %param.12, s32[1024]{0:T(1024)S(1)} %pad_clamp_fusion), kind=kCustom, calls=%fused_computation.3 | custom fusion | bytes 7340064 | tf_op jit(solution)/shard_map/jit(_take)/gather | solution.py:34
  86.6 53.9 %all-gather.5.cloned.1.call-done = bf16[8,8,64,2048]{3,2,1,0:T(8,128)(2,1)} async-done(((bf16[1,8,64,2048]{3,2,1,0:T(8,128)(2,1)}), bf16[8,8,64,2048]{3,2,1,0:T(8,128)(2,1)}) %all-gather.5.cloned.1.call-update) | async-done | bytes 16777232 | tf_op jit(solution)/shard_map/all_gather | solution.py:32
  140.5 10.0 %reduce_sum.25 = bf16[8,64,2048]{2,1,0:T(8,128)(2,1)S(1)} reduce(bf16[8,8,64,2048]{3,2,1,0:T(8,128)(2,1)} %all-gather.5.cloned.1.call-done, bf16[]{:T(256)} %constant.121.clone.1), dimensions={0}, to_apply=%region_3.4 | reduce | flops 7340032 | bytes 18874370 | tf_op jit(solution)/shard_map/reduce_sum | solution.py:32
  150.4 3.8 fusion.6
  154.2 0.2 copy.16
  154.4 0.8 convert_element_type.61
  155.2 0.0 all-reduce.2.cloned.1.call-update
  155.2 0.2 reduce-scatter.5.cloned.1.call-start
  155.5 4.9 %select_convert_fusion = bf16[8,2,64,1792]{3,2,1,0:T(8,128)(2,1)} fusion(bf16[8,2,64,1792]{3,2,1,0:T(8,128)(2,1)} %gather_fusion.3, pred[8]{0:T(512)(128)(4,1)S(1)} %get-tuple-element.10, pred[8]{0:T(512)(128)(4,1)S(1)} %get-tuple-element.11), kind=kLoop, calls=%fused_computation.5 | loop fusion | flops 7340032 | bytes 7340048 | tf_op jit(solution)/shard_map/convert_element_type | solution.py:37
  160.4 0.0 reduce-scatter.5.cloned.1.call-update
  160.4 110.1 %reduce-scatter.3.cloned.1.call-done = bf16[256,3584]{1,0:T(8,128)(2,1)} async-done(((bf16[1024,3584]{1,0:T(8,128)(2,1)}), bf16[256,3584]{1,0:T(8,128)(2,1)}) %reduce-scatter.3.cloned.1.call-update) | async-done | bytes 1835024 | tf_op jit(solution)/shard_map/reduce_scatter | solution.py:55
  270.6 3.7 convert_element_type.55
  274.3 33.5 %all-reduce.2.cloned.1.call-done = bf16[512,128]{1,0:T(8,128)(2,1)} async-done(((bf16[512,128]{1,0:T(8,128)(2,1)}), bf16[512,128]{1,0:T(8,128)(2,1)}) %all-reduce.2.cloned.1.call-update) | async-done | bytes 131088 | tf_op jit(solution)/shard_map/psum | solution.py:49
  307.7 0.8 convert_convert_fusion
  308.5 0.1 reshape.311
  308.6 69.5 %reduce-scatter.5.cloned.1.call-done = bf16[2,2,64,1792]{3,2,1,0:T(8,128)(2,1)} async-done(((bf16[8,2,64,1792]{3,2,1,0:T(8,128)(2,1)}), bf16[2,2,64,1792]{3,2,1,0:T(8,128)(2,1)}) %reduce-scatter.5.cloned.1.call-update) | async-done | bytes 917520 | tf_op jit(solution)/shard_map/reduce_scatter | solution.py:36
  378.1 0.0 copy-start.2
  378.1 1.9 fusion.7
  380.0 0.0 copy-start.1
  380.0 0.4 copy-done.2
  380.4 1.5 fusion.3
  381.9 0.0 copy-done.1
  (10 shorter events, 0.1 us)
Async XLA Ops:
  6.5 4.4 %copy-start = (bf16[8,64,2048]{2,1,0:T(8,128)(2,1)S(1)}, bf16[8,64,2048]{2,1,0:T(8,128)(2,1)}, u32[]{:S(2)}) copy-start(bf16[8,64,2048]{2,1,0:T(8,128)(2,1)} %param.11) | copy-start | bytes 6291460
  6.5 42.2 %all-gather.3.cloned.1.call-start = ((), (), s32[]{:S(2)}) async-start(), calls=%async_computation.2 | async-start | bytes 4718592 | tf_op jit(solution)/shard_map/all_gather | solution.py:39
  7.3 133.2 %all-gather.5.cloned.1.call-start = ((), (), s32[]{:S(2)}) async-start(), calls=%async_computation.4 | async-start | bytes 18874368 | tf_op jit(solution)/shard_map/all_gather | solution.py:32
  16.7 253.9 %reduce-scatter.3.cloned.1.call-start = ((), (), s32[]{:S(2)}) async-start(), calls=%async_computation.3 | async-start | bytes 9175040 | tf_op jit(solution)/shard_map/reduce_scatter | solution.py:55
  48.7 13.0 %copy-start.3 = (bf16[1024,2048]{1,0:T(8,128)(2,1)S(1)}, bf16[1024,2048]{1,0:T(8,128)(2,1)}, u32[]{:S(2)}) copy-start(bf16[1024,2048]{1,0:T(8,128)(2,1)} %all-gather.3.cloned.1.call-done) | copy-start | bytes 12582916
  80.8 227.0 %all-reduce.2.cloned.1.call-start = ((), (), s32[]{:S(2)}) async-start(), calls=%async_computation.5 | async-start | bytes 262144 | tf_op jit(solution)/shard_map/psum | solution.py:49
  155.2 222.8 %reduce-scatter.5.cloned.1.call-start = ((), (), s32[]{:S(2)}) async-start(), calls=%async_computation.6 | async-start | bytes 4587520 | tf_op jit(solution)/shard_map/reduce_scatter | solution.py:36
  378.1 2.3 copy-start.2
  380.0 1.9 copy-start.1
Sparse Core Ops, SparseCore 0:
  9.2 39.4 all-gather.2
  50.6 89.8 all-gather.4
  142.8 127.7 reduce-scatter.2
  272.7 34.9 all-reduce.1
  310.0 68.0 reduce-scatter.4
